TPU v7x, 32 devices: a whole 2x2x4 slice. The times are simulated.
32 devices in a mesh: band: 4 (over y, core), mem: 8 (over z, x).
Axes of the slice: x: 2, y: 2, z: 4, core: 2. Of those that a mesh axis runs over, the one named last changes fastest.
Arguments:
- latent: bfloat16 [8, 32, 512, 512], P('mem', 'band'), may hold values from -6 to 6
- truth: float32 [80, 32, 512], P(None, 'band', 'mem'), may hold values from -6 to 6
- node_weight: float32 [32, 512], P('band', 'mem'), may hold values from 0.25 to 1
- first_weight: bfloat16 [512, 512], replicated, may hold values from -0.25 to 0.25
- first_bias: float32 [512], replicated, may hold values from -3 to 3
- second_weight: bfloat16 [512, 512], replicated, may hold values from -0.25 to 0.25
- second_bias: float32 [512], replicated, may hold values from -3 to 3
- out_weight: bfloat16 [80, 512], replicated, may hold values from -0.25 to 0.25
- out_bias: float32 [80], replicated, may hold values from -3 to 3
Outputs:
- score: float32 [32, 512], P('band', 'mem')
- grad_first_weight: float32 [512, 512], P('mem')
- grad_first_bias: float32 [512], replicated
- grad_second_weight: float32 [512, 512], P('mem')
- grad_second_bias: float32 [512], replicated
- grad_out_weight: float32 [80, 512], replicated
- grad_out_bias: float32 [80], replicated
All inputs are finite; a program needn't handle non-finite values.
Results may differ from a plain program's by a relative error of at most 0.0014.
Values sent between devices are 32-bit elements; how exact they have to be, the bound alone decides.
A program may use at most 128 MiB of HBM per device.

v0:
```python
import functools
import math
import jax
import jax.numpy as jnp
from jax import lax
from jax.experimental import pallas as pl
from jax.experimental.pallas import tpu as pltpu
from jax.sharding import PartitionSpec as P

RADIUS = 3
LANES = 128
MESH = pl.DeviceIdType.MESH

root_half = 0.7071067811865476
density_scale = 0.3989422804014327
tap_spread = 1.5
epsilon = 1e-06


def gelu_pair(value):
    normal_cdf = 0.5 * (1.0 + lax.erf(value * root_half))
    return (value * normal_cdf, normal_cdf + value * jnp.exp(-0.5 * value * value) * density_scale)


def stencil_taps(radius):
    weights = [math.exp(-k * k / (2.0 * tap_spread * tap_spread)) for k in range(-radius, radius + 1)]
    return [w / sum(weights) for w in weights]


def remote(src, dst, send, recv, where):
    return pltpu.make_async_remote_copy(
        src_ref=src, dst_ref=dst, send_sem=send, recv_sem=recv, device_id=where, device_id_type=MESH
    )


def peer(me, p, count):
    if count & (count - 1):
        return lax.rem(me + p, count)
    total, bit = 0, 1
    while bit < count:
        total = total + lax.rem(me // bit + p // bit, 2) * bit
        bit *= 2
    return total


def smooth_block(before, own, after, taps, cols):
    edge, length = before.shape[1], own.shape[1]
    padded = jnp.concatenate([before, own, after], axis=1)
    width = padded.shape[1]
    rolled = {0: padded}
    total = None
    for index, tap in enumerate(taps):
        shift = (index - RADIUS) * cols
        rest = shift % LANES
        if rest not in rolled:
            rolled[rest] = pltpu.roll(padded, width - rest, 1)
        start = edge + shift - rest
        term = tap * rolled[rest][:, start : start + length]
        total = term if total is None else total + term
    return total


def contract(left, right, left_dim, right_dim):
    return lax.dot_general(
        left, right, (((left_dim,), (right_dim,)), ((), ())), preferred_element_type=jnp.float32
    )


def reduce_in_kernel(
    members, bands, rows, g_ref, shares, small_all,
    first, held, second, quarter, third, pair, fourth, final_s, gather_w, gather_s, gather_b,
    s1, r1, s2, r2, s3, r3, s4, r4, s5, r5, s6, r6, s7, r7,
):
    me = lax.axis_index("mem")
    band = lax.axis_index("band")
    low, high = lax.rem(band, 2), band // 2
    half, part = g_ref.shape[2] // 2, g_ref.shape[2] // bands
    partner = {"band": high * 2 + 1 - low}
    across = {"band": (1 - high) * 2 + low}
    def cut(index, size):
        return pl.ds(pl.multiple_of(index * size, size), size)

    def one(k):
        return remote(g_ref.at[k, :, cut(1 - low, half)], first.at[k], s1.at[k], r1.at[k], partner)

    def two(k):
        return remote(held.at[k, :, cut(1 - high, part)], second.at[k], s2.at[k], r2.at[k], across)

    parity = lax.rem(me, 2)
    beside = {"mem": me + 1 - 2 * parity}
    groups = members // 2

    def three(q):
        k = 2 * q + 1 - parity
        return remote(quarter.at[k], third.at[q], s3.at[q], r3.at[q], beside)

    def four(q):
        return remote(pair.at[q], fourth.at[me // 2], s7.at[q], r7.at[me // 2], {"mem": 2 * q + parity})

    def arrived(buffer, sems, k):
        remote(buffer.at[k], buffer.at[k], sems.at[k], sems.at[k], {"mem": k}).wait_recv()

    def step_one(p, carry):
        one(peer(me, members - p, members)).start()
        return carry

    def step_two(p, carry):
        k = peer(me, members - p, members)
        one(k).wait_recv()
        held[k] = g_ref[k, :, cut(low, half)] + first[k]
        two(k).start()
        return carry

    def step_three(p, carry):
        k = peer(me, members - p, members)
        two(k).wait_recv()
        quarter[k] = held[k, :, cut(high, part)] + second[k]

        @pl.when(lax.rem(k, 2) != parity)
        def _():
            three(k // 2).start()

        return carry

    def step_four(p, carry):
        q = peer(me // 2, groups - p, groups)
        three(q).wait_recv()
        pair[q] = quarter[2 * q + parity] + third[q]

        @pl.when(p < groups)
        def _():
            four(q).start()

        return carry

    lax.fori_loop(1, members + 1, step_one, 0)
    lax.fori_loop(1, members + 1, step_two, 0)
    lax.fori_loop(1, members + 1, step_three, 0)
    lax.fori_loop(1, groups + 1, step_four, 0)

    def gather(p, total):
        q = peer(me // 2, p, groups)
        remote(fourth.at[q], fourth.at[q], s7.at[q], r7.at[q], {"mem": 2 * q + parity}).wait_recv()
        return total + fourth[q]

    total = lax.fori_loop(1, groups, gather, pair[me // 2])
    final_s[...] = total[2 * rows :]
    gather_w[band] = total[: 2 * rows]
    gather_s[me] = total[2 * rows :]

    def small(k):
        return remote(final_s, gather_s.at[me], s4.at[k], r4.at[me], {"mem": k})

    def weights(slot, who, where):
        return remote(gather_w.at[slot], gather_w.at[slot], s5.at[who], r5.at[slot], where)

    def smalls(slot, who, where):
        return remote(gather_b.at[slot], gather_b.at[slot], s6.at[who], r6.at[slot], where)

    far = (1 - high) * 2 + low
    near = high * 2 + 1 - low
    near_far = (1 - high) * 2 + 1 - low

    def send_small(p, carry):
        small(peer(me, members - p, members)).start()
        return carry

    lax.fori_loop(1, members, send_small, 0)
    weights(band, 0, across).start()
    weights(band, 1, partner).start()

    def take_small(p, carry):
        arrived(gather_s, r4, peer(me, p, members))
        return carry

    lax.fori_loop(1, members, take_small, 0)
    gather_b[band] = gather_s[...]
    smalls(band, 0, across).start()
    smalls(band, 1, partner).start()
    weights(far, 2, across).wait_recv()
    weights(far, 2, partner).start()
    smalls(far, 2, across).wait_recv()
    smalls(far, 2, partner).start()
    for slot in (near, near_far):
        weights(slot, 0, partner).wait_recv()
        smalls(slot, 0, partner).wait_recv()
    for k in range(bands):
        lanes = slice((k % 2) * half + (k // 2) * part, (k % 2) * half + (k // 2) * part + part)
        shares[:, lanes] = gather_w[k]
        small_all[:, lanes] = gather_b[k].reshape(small_all.shape[0], part)
    for slot, who, where in ((band, 0, across), (band, 1, partner), (far, 2, partner)):
        weights(slot, who, where).wait_send()
        smalls(slot, who, where).wait_send()

    def drain(k, carry):
        one(k).wait_send()
        two(k).wait_send()

        @pl.when(k != me)
        def _():
            small(k).wait_send()

        return carry

    def drain_groups(q, carry):
        three(q).wait_send()

        @pl.when(q != me // 2)
        def _():
            four(q).wait_send()

        return carry

    lax.fori_loop(0, members, drain, 0)
    lax.fori_loop(0, groups, drain_groups, 0)


def score_kernel(
    members, bands, cols, edge,
    latent_ref, first_ref, first_bias_ref, second_ref, second_bias_ref, out_weight_ref, out_bias_ref,
    truth_ref, node_ref,
    score_out, first_out, first_bias_out, second_out, second_bias_out, out_weight_out, out_bias_out,
    rows_in, first_act, first_slope, second_act, second_slope, first_sum, second_sum, small_sum, bias_sum, raw_ref,
    before, after, grad_before, grad_after, sent, ensemble, grads, back,
    halo_send, halo_recv, fwd_send, fwd_recv, ret_send, ret_recv, ghalo_send, ghalo_recv, load,
    score_ref, weight_ref, bias_column, g_ref, shares, small_all, *reduce_refs,
):
    me = lax.axis_index("mem")
    band = lax.axis_index("band")
    length = raw_ref.shape[2]
    rows = first_out.shape[0]
    taps = stencil_taps(RADIUS)
    has_prev = band > 0
    has_next = band < bands - 1
    prev, following = jnp.maximum(band - 1, 0), jnp.minimum(band + 1, bands - 1)

    def fetch(k):
        where = pl.ds(pl.multiple_of(k * cols, cols), cols)
        return pltpu.make_async_copy(latent_ref.at[:, where, :], rows_in.at[k], load.at[k])

    def prefetch(p, carry):
        fetch(peer(me, members - p, members)).start()
        return carry

    lax.fori_loop(1, members + 1, prefetch, 0)
    barrier = pltpu.get_barrier_semaphore()

    def greet(p, carry):
        pl.semaphore_signal(barrier, inc=1, device_id={"mem": peer(me, members - p, members)}, device_id_type=MESH)
        return carry

    lax.fori_loop(1, members, greet, 0)

    for d in range(1, bands):
        pl.semaphore_signal(barrier, inc=1, device_id={"band": lax.rem(band + d, bands)}, device_id_type=MESH)
    channels, hidden = out_weight_ref.shape
    shape = (channels, channels)
    diagonal = lax.broadcasted_iota(jnp.int32, shape, 0) == lax.broadcasted_iota(jnp.int32, shape, 1)
    bias_column[...] = jnp.sum(jnp.where(diagonal, out_bias_ref[...], 0.0), axis=1, keepdims=True)
    for row in range(node_ref.shape[0]):
        weight_ref[:, row * cols : (row + 1) * cols] = node_ref[row : row + 1, :]
    pl.semaphore_wait(barrier, members + bands - 2)

    @pl.when(band == 0)
    def _():
        before[...] = jnp.zeros_like(before)
        grad_before[...] = jnp.zeros_like(grad_before)

    @pl.when(band == bands - 1)
    def _():
        after[...] = jnp.zeros_like(after)
        grad_after[...] = jnp.zeros_like(grad_after)

    def to_next(source, target, k, send, recv):
        return remote(source.at[k, :, pl.ds(length - edge, edge)], target.at[k], send.at[0, k], recv.at[0, k], {"band": following})

    def to_prev(source, target, k, send, recv):
        return remote(source.at[k, :, pl.ds(0, edge)], target.at[k], send.at[1, k], recv.at[1, k], {"band": prev})

    def start_edges(source, low, high, k, send, recv):
        @pl.when(has_next)
        def _():
            to_next(source, low, k, send, recv).start()

        @pl.when(has_prev)
        def _():
            to_prev(source, high, k, send, recv).start()

    def wait_edges(source, low, high, k, send, recv):
        @pl.when(has_prev)
        def _():
            to_next(source, low, k, send, recv).wait_recv()

        @pl.when(has_next)
        def _():
            to_prev(source, high, k, send, recv).wait_recv()

    def drain_edges(source, low, high, k, send, recv):
        @pl.when(has_next)
        def _():
            to_next(source, low, k, send, recv).wait_send()

        @pl.when(has_prev)
        def _():
            to_prev(source, high, k, send, recv).wait_send()

    raw_edges = (raw_ref, before, after)
    grad_edges = (back, grad_before, grad_after)

    def forward(k):
        return remote(sent.at[k], ensemble.at[me], fwd_send.at[k], fwd_recv.at[me], {"mem": k})

    def returning(k):
        return remote(grads.at[k], back.at[me], ret_send.at[k], ret_recv.at[me], {"mem": k})

    def arrived(buffer, sems, k):
        remote(buffer.at[k], buffer.at[k], sems.at[k], sems.at[k], {"mem": k}).wait_recv()

    def decode(k):
        fetch(k).wait()
        inputs = rows_in[k].reshape(length, rows_in.shape[3])
        pre = jnp.dot(inputs, first_ref[...], preferred_element_type=jnp.float32) + first_bias_ref[...]
        act, slope = gelu_pair(pre)
        first_act[k] = act.astype(jnp.bfloat16)
        first_slope[k] = slope
        pre = jnp.dot(first_act[k], second_ref[...], preferred_element_type=jnp.float32) + second_bias_ref[...]
        act, slope = gelu_pair(pre)
        second_act[k] = act.astype(jnp.bfloat16)
        second_slope[k] = slope
        raw_ref[k] = contract(out_weight_ref[...], second_act[k], 1, 1) + bias_column[...]

    def spread(p):
        k = peer(me, members - p, members)
        wait_edges(*raw_edges, k, halo_send, halo_recv)
        smooth = smooth_block(before[k], raw_ref[k], after[k], taps, cols)

        @pl.when(p < members)
        def _():
            sent[k] = smooth
            forward(k).start()

        @pl.when(p == members)
        def _():
            ensemble[k] = smooth

    def forward_step(p, carry):
        @pl.when(p <= members)
        def _():
            k = peer(me, members - p, members)
            decode(k)
            start_edges(*raw_edges, k, halo_send, halo_recv)

        @pl.when(p >= 2)
        def _():
            spread(p - 1)

        return carry

    lax.fori_loop(1, members + 2, forward_step, 0)

    def collect(p, carry):
        arrived(ensemble, fwd_recv, peer(me, p, members))
        return carry

    lax.fori_loop(1, members, collect, 0)
    score_ref[...] = jnp.zeros_like(score_ref)
    pair_count = members * (members - 1)
    row_ids = lax.broadcasted_iota(jnp.int32, (members, LANES), 0)

    def member(p, carry):
        m = peer(me, members - p, members)

        def chunk(c, inner):
            lanes = pl.ds(pl.multiple_of(c * LANES, LANES), LANES)
            mine = ensemble[m, :, lanes]
            gaps = mine[None] - ensemble[:, :, lanes]
            distance = jnp.sqrt(jnp.sum(gaps * gaps, axis=1) + epsilon)
            own = row_ids == m
            inverse = jnp.where(own, 0.0, 1.0 / distance)
            spread_sum = jnp.sum(jnp.where(own, 0.0, distance), axis=0, keepdims=True)
            pair_grad = jnp.sum(gaps * inverse[:, None, :], axis=0)
            error = mine - truth_ref[:, lanes]
            skill = jnp.sqrt(jnp.sum(error * error, axis=0, keepdims=True) + epsilon)
            score_ref[:, lanes] += skill / members - spread_sum / (2.0 * pair_count)
            result = weight_ref[:, lanes] * (error / (members * skill) - pair_grad / pair_count)

            @pl.when(p < members)
            def _():
                grads[m, :, lanes] = result

            @pl.when(p == members)
            def _():
                back[m, :, lanes] = result

            return inner

        lax.fori_loop(0, length // LANES, chunk, 0)

        @pl.when(p < members)
        def _():
            returning(m).start()

        return carry

    lax.fori_loop(1, members + 1, member, 0)
    start_edges(*grad_edges, me, ghalo_send, ghalo_recv)

    first_sum[...] = jnp.zeros_like(first_sum)
    second_sum[...] = jnp.zeros_like(second_sum)
    small_sum[...] = jnp.zeros_like(small_sum)
    bias_sum[...] = jnp.zeros_like(bias_sum)

    def finish(p):
        k = peer(me, p, members)
        wait_edges(*grad_edges, k, ghalo_send, ghalo_recv)
        grad_raw = smooth_block(grad_before[k], back[k], grad_after[k], taps, cols)
        grad_low = grad_raw.astype(jnp.bfloat16)
        bias_sum[...] += jnp.sum(grad_raw, axis=1, keepdims=True)
        small_sum[:channels] += jnp.dot(grad_low, second_act[k], preferred_element_type=jnp.float32)
        delta = contract(grad_low, out_weight_ref[...], 0, 0) * second_slope[k]
        small_sum[channels + 1 : channels + 2] += jnp.sum(delta, axis=0, keepdims=True)
        low = delta.astype(jnp.bfloat16)
        second_sum[...] += contract(first_act[k], low, 0, 0)
        delta = contract(low, second_ref[...], 1, 1) * first_slope[k]
        small_sum[channels : channels + 1] += jnp.sum(delta, axis=0, keepdims=True)
        inputs = rows_in[k].reshape(length, rows_in.shape[3])
        first_sum[...] += contract(inputs, delta.astype(jnp.bfloat16), 0, 0)

    def backward_step(p, carry):
        @pl.when(p < members)
        def _():
            k = peer(me, p, members)
            arrived(back, ret_recv, k)
            start_edges(*grad_edges, k, ghalo_send, ghalo_recv)

        finish(p - 1)
        return carry

    lax.fori_loop(1, members + 1, backward_step, 0)
    small_sum[channels + 2 : channels + 3, :channels] = jnp.sum(
        jnp.where(diagonal, bias_sum[...], 0.0), axis=0, keepdims=True
    )
    g_ref[:, :rows] = first_sum[...].reshape(members, rows, hidden)
    g_ref[:, rows : 2 * rows] = second_sum[...].reshape(members, rows, hidden)
    g_ref[:, 2 * rows :] = small_sum[...].reshape(members, -1, hidden)
    reduce_in_kernel(members, bands, rows, g_ref, shares, small_all, *reduce_refs)
    for row in range(score_out.shape[0]):
        score_out[row : row + 1, :] = score_ref[:, row * cols : (row + 1) * cols]
    first_out[...] = shares[:rows]
    second_out[...] = shares[rows:]
    out_weight_out[...] = small_all[:channels]
    first_bias_out[...] = small_all[channels : channels + 1]
    second_bias_out[...] = small_all[channels + 1 : channels + 2]
    out_bias_out[...] = small_all[channels + 2 : channels + 3, :channels]

    def drain(k, carry):
        drain_edges(*raw_edges, k, halo_send, halo_recv)
        drain_edges(*grad_edges, k, ghalo_send, ghalo_recv)

        @pl.when(k != me)
        def _():
            forward(k).wait_send()
            returning(k).wait_send()

        return carry

    lax.fori_loop(0, members, drain, 0)


def score_and_gradient(latent, weights, truth, weight, members, bands, cols, rows, extra):
    lat_rows, _, features = latent.shape
    channels, length = truth.shape
    hidden = weights[0].shape[1]
    edge = min(length, -(-RADIUS * cols // LANES) * LANES)
    height, part = 2 * rows + extra, hidden // bands
    block = (members, channels, length)
    halo = (members, channels, edge)
    units = (members, length, hidden)
    dma = pltpu.SemaphoreType.DMA
    vmem = pl.BlockSpec(memory_space=pltpu.VMEM)
    single, half = jnp.float32, jnp.bfloat16
    return pl.pallas_call(
        functools.partial(score_kernel, members, bands, cols, edge),
        out_shape=tuple(
            jax.ShapeDtypeStruct(o, single)
            for o in (
                (lat_rows, cols), (rows, hidden), (1, hidden), (rows, hidden), (1, hidden),
                (channels, hidden), (1, channels),
            )
        ),
        in_specs=[pl.BlockSpec(memory_space=pl.ANY)] + [vmem] * 8,
        out_specs=(vmem,) * 7,
        scratch_shapes=[
            pltpu.VMEM((members, lat_rows, cols, features), half),
            pltpu.VMEM(units, half), pltpu.VMEM(units, single),
            pltpu.VMEM(units, half), pltpu.VMEM(units, single),
            pltpu.VMEM((features, hidden), single), pltpu.VMEM((hidden, hidden), single),
            pltpu.VMEM((members * extra, hidden), single), pltpu.VMEM((channels, 1), single),
            pltpu.VMEM(block, single),
        ]
        + [pltpu.VMEM(halo, single)] * 4
        + [pltpu.VMEM(block, single)] * 4
        + [dma((2, members))] * 2
        + [dma((members,))] * 4
        + [dma((2, members))] * 2
        + [dma((members,))]
        + [pltpu.VMEM(o, single) for o in [
            (1, length), (1, length), (channels, 1),
            (members, height, hidden), (2 * rows, hidden), (members * extra, hidden),
            (members, height, hidden // 2), (members, height, hidden // 2),
            (members, height, part), (members, height, part),
            (members // 2, height, part), (members // 2, height, part), (members // 2, height, part),
            (extra, part), (bands, 2 * rows, part), (members, extra, part), (bands, members, extra, part),
        ]]
        + [dma((n,)) for n in [members] * 4 + [members // 2] * 2 + [members] * 2]
        + [dma((n,)) for n in [bands] * 4 + [members // 2] * 2],
        compiler_params=pltpu.CompilerParams(collective_id=0, has_side_effects=True, vmem_limit_bytes=60 << 20),
    )(latent, *weights, truth, weight)


def write_kernel(*refs):
    count = len(refs) // 2
    for source, target in zip(refs[:count], refs[count:]):
        target[...] = source[...]


def write_results(values):
    vmem = pl.BlockSpec(memory_space=pltpu.VMEM)
    return pl.pallas_call(
        write_kernel,
        out_shape=tuple(jax.ShapeDtypeStruct(v.shape, v.dtype) for v in values),
        in_specs=[vmem] * len(values),
        out_specs=(vmem,) * len(values),
    )(*values)


def body(
    latent, truth, node_weight, first_weight, first_bias, second_weight, second_bias, out_weight, out_bias
):
    members, bands = lax.axis_size("mem"), lax.axis_size("band")
    _, lat_rows, lon_cols, features = latent.shape
    channels, hidden = out_weight.shape
    cols = lon_cols // members
    rows = features // members
    extra = -(-(channels + 3) // (8 * members)) * 8
    weights = (
        first_weight, first_bias[None], second_weight, second_bias[None], out_weight, out_bias[None]
    )
    score, first, first_b, second, second_b, out_w, out_b = write_results(score_and_gradient(
        latent.reshape(lat_rows, lon_cols, features), weights,
        truth.reshape(channels, -1), node_weight, members, bands, cols, rows, extra,
    ))
    return (score, first, first_b[0], second, second_b[0], out_w, out_b[0])


def solution(mesh):
    in_specs = (
        P("mem", "band", None, None),
        P(None, "band", "mem"),
        P("band", "mem"),
        P(),
        P(),
        P(),
        P(),
        P(),
        P(),
    )
    out_specs = (P("band", "mem"), P("mem", None), P(), P("mem", None), P(), P(), P())
    return jax.shard_map(body, mesh=mesh, in_specs=in_specs, out_specs=out_specs, check_vma=False)
```

profile of v0, /device:TPU:0, one launch (start us, length us, event | category | flops | bytes accessed | tf_op | source)
XLA Modules:
  0.0 117.6 jit_solution(844857488445059473)
XLA Ops:
  0.6 1.7 %copy.18.truth_ref = f32[80,512]{1,0:T(8,128)} copy(f32[80,512]{0,1:T(8,128)} %bitcast.9) | data formatting | bytes 327680 | tf_op jit(solution)/shard_map/reshape | solution.py:551
  2.4 113.4 %shard_map.144 = (f32[8,64]{1,0:T(8,128)}, f32[64,512]{1,0:T(8,128)}, f32[1,512]{1,0:T(1,128)}, f32[64,512]{1,0:T(8,128)}, f32[1,512]{1,0:T(1,128)}, /*index=5*/f32[80,512]{1,0:T(8,128)}, f32[1,80]{1,0:T(1,128)}) custom-call(bf16[8,512,512]{2,1,0:T(8,128)(2,1)} %bitcast.8, bf16[512,512]{1,0:T(8,128)(2,1)} %first_ref.1, f32[1,512]{1,0:T(1,128)} %bitcast.10, ...), custom_call_target="tpu_custom_call" | custom-call | tf_op jit(solution)/shard_map/pallas_call | solution.py:482
  115.8 1.8 %shard_map.145 = (f32[8,64]{1,0:T(8,128)}, f32[64,512]{1,0:T(8,128)}, f32[1,512]{1,0:T(1,128)}, f32[64,512]{1,0:T(8,128)}, f32[1,512]{1,0:T(1,128)}, /*index=5*/f32[80,512]{1,0:T(8,128)}, f32[1,80]{1,0:T(1,128)}) custom-call(f32[8,64]{1,0:T(8,128)} %get-tuple-element.21.refs_0_, f32[64,512]{1,0:T(8,128)} %get-tuple-element.22.refs_1_, ...), custom_call_target="tpu_custom_call" | custom-call | tf_op jit(solution)/shard_map/pallas_call | solution.py:529
where the time goes:
time: 118 us
  Pallas kernels  115 us (97%)
  local copies, waits for them, and re-layouts  1.74 us (1%)
    pallas_call x1, Pallas kernels, score_and_gradient(): pl.pallas_call(functools.partial(score_kernel, members, bands, cols, edge...  113 us

commit v1 on v0

--- a/solution.py
+++ b/solution.py
@@ -67,163 +67,260 @@
 
 
 def reduce_in_kernel(
-    members, bands, rows, g_ref, shares, small_all,
-    first, held, second, quarter, third, pair, fourth, final_s, gather_w, gather_s, gather_b,
-    s1, r1, s2, r2, s3, r3, s4, r4, s5, r5, s6, r6, s7, r7,
+    members, bands, first_sum, second_sum, small_sum, first_out, second_out, small_all,
+    core_in, held, y_in, y_sum, x_wide, x_sum, x_in, y_late, pair, z_in, gather_w,
+    t_core, t_held, t_y, t_ysum, t_x, t_xsum, t_z, final_s, gather_s, gather_b,
+    sc, rc, sy, ry, sx, rx, sxw, rxw, syl, ryl, sz, rz, st, rt, stz, rtz, stg, rtg, sgw, rgw, sgb, rgb,
 ):
     me = lax.axis_index("mem")
     band = lax.axis_index("band")
     low, high = lax.rem(band, 2), band // 2
-    half, part = g_ref.shape[2] // 2, g_ref.shape[2] // bands
+    parity, group = lax.rem(me, 2), me // 2
+    groups = members // 2
+    rows = first_out.shape[0]
+    hidden = first_sum.shape[1]
+    half, part = hidden // 2, hidden // bands
+    extra = final_s.shape[0]
     partner = {"band": high * 2 + 1 - low}
     across = {"band": (1 - high) * 2 + low}
+    beside = {"mem": me + 1 - 2 * parity}
+
     def cut(index, size):
         return pl.ds(pl.multiple_of(index * size, size), size)
 
-    def one(k):
-        return remote(g_ref.at[k, :, cut(1 - low, half)], first.at[k], s1.at[k], r1.at[k], partner)
-
-    def two(k):
-        return remote(held.at[k, :, cut(1 - high, part)], second.at[k], s2.at[k], r2.at[k], across)
-
-    parity = lax.rem(me, 2)
-    beside = {"mem": me + 1 - 2 * parity}
-    groups = members // 2
-
-    def three(q):
-        k = 2 * q + 1 - parity
-        return remote(quarter.at[k], third.at[q], s3.at[q], r3.at[q], beside)
-
-    def four(q):
-        return remote(pair.at[q], fourth.at[me // 2], s7.at[q], r7.at[me // 2], {"mem": 2 * q + parity})
-
-    def arrived(buffer, sems, k):
-        remote(buffer.at[k], buffer.at[k], sems.at[k], sems.at[k], {"mem": k}).wait_recv()
-
-    def step_one(p, carry):
-        one(peer(me, members - p, members)).start()
-        return carry
-
-    def step_two(p, carry):
-        k = peer(me, members - p, members)
-        one(k).wait_recv()
-        held[k] = g_ref[k, :, cut(low, half)] + first[k]
-        two(k).start()
-        return carry
-
-    def step_three(p, carry):
-        k = peer(me, members - p, members)
-        two(k).wait_recv()
-        quarter[k] = held[k, :, cut(high, part)] + second[k]
-
-        @pl.when(lax.rem(k, 2) != parity)
-        def _():
-            three(k // 2).start()
-
-        return carry
-
-    def step_four(p, carry):
-        q = peer(me // 2, groups - p, groups)
-        three(q).wait_recv()
-        pair[q] = quarter[2 * q + parity] + third[q]
-
-        @pl.when(p < groups)
-        def _():
-            four(q).start()
-
-        return carry
-
-    lax.fori_loop(1, members + 1, step_one, 0)
-    lax.fori_loop(1, members + 1, step_two, 0)
-    lax.fori_loop(1, members + 1, step_three, 0)
-    lax.fori_loop(1, groups + 1, step_four, 0)
-
-    def gather(p, total):
-        q = peer(me // 2, p, groups)
-        remote(fourth.at[q], fourth.at[q], s7.at[q], r7.at[q], {"mem": 2 * q + parity}).wait_recv()
-        return total + fourth[q]
-
-    total = lax.fori_loop(1, groups, gather, pair[me // 2])
-    final_s[...] = total[2 * rows :]
-    gather_w[band] = total[: 2 * rows]
-    gather_s[me] = total[2 * rows :]
-
-    def small(k):
-        return remote(final_s, gather_s.at[me], s4.at[k], r4.at[me], {"mem": k})
-
-    def weights(slot, who, where):
-        return remote(gather_w.at[slot], gather_w.at[slot], s5.at[who], r5.at[slot], where)
-
-    def smalls(slot, who, where):
-        return remote(gather_b.at[slot], gather_b.at[slot], s6.at[who], r6.at[slot], where)
+    mine, other = cut(high, part), cut(1 - high, part)
+
+    def both(q):
+        return cut(q, 2 * rows)
+
+    def kept(q):
+        return cut(2 * q + parity, rows)
+
+    def given(q):
+        return cut(2 * q + 1 - parity, rows)
+
+    def core(w, q):
+        source = (second_sum, first_sum)[w]
+        return remote(
+            source.at[both(q), cut(1 - low, half)], core_in.at[w, both(q)], sc.at[w, q], rc.at[w, q], partner
+        )
+
+    def along_y(q):
+        return remote(held.at[0, both(q), other], y_in.at[both(q)], sy.at[q], ry.at[q], across)
+
+    def along_x(q):
+        return remote(y_sum.at[given(q)], x_in.at[q], sx.at[q], rx.at[q], beside)
+
+    def wide_x(q):
+        return remote(held.at[1, given(q)], x_wide.at[q], sxw.at[q], rxw.at[q], beside)
+
+    def late_y(q):
+        return remote(x_sum.at[q, :, other], y_late.at[q], syl.at[q], ryl.at[q], across)
+
+    def along_z(q):
+        return remote(pair.at[q], z_in.at[group], sz.at[q], rz.at[group], {"mem": 2 * q + parity})
+
+    small_core = remote(small_sum.at[:, cut(1 - low, half)], t_core, st.at[0], rt.at[0], partner)
+    small_y = remote(t_held.at[:, other], t_y, st.at[1], rt.at[1], across)
+    spread = groups * extra
+    small_x = remote(t_ysum.at[cut(1 - parity, spread)], t_x, st.at[2], rt.at[2], beside)
+    slot = parity * groups + group
+
+    def small_z(q):
+        return remote(t_xsum.at[cut(q, extra)], t_z.at[group], stz.at[q], rtz.at[group], {"mem": 2 * q + parity})
+
+    def slot_of(k):
+        return lax.rem(k, 2) * groups + k // 2
+
+    def small_gather(k):
+        return remote(final_s, gather_s.at[slot], stg.at[k], rtg.at[me], {"mem": k})
+
+    def step_core(t, carry):
+        q = peer(group, groups - 1 - t, groups)
+        core(0, q).start()
+        core(1, q).start()
+        return carry
+
+    small_core.start()
+    lax.fori_loop(0, groups, step_core, 0)
+    small_core.wait_recv()
+    t_held[...] = small_sum[:, cut(low, half)] + t_core[...]
+    small_y.start()
+
+    def near(index):
+        return peer(group, groups - 1 - index, groups)
+
+    def step(t, carry):
+        @pl.when(t < groups)
+        def _():
+            q = near(t)
+            core(0, q).wait_recv()
+            held[0, both(q)] = second_sum[both(q), cut(low, half)] + core_in[0, both(q)]
+            along_y(q).start()
+            core(1, q).wait_recv()
+            held[1, both(q)] = first_sum[both(q), cut(low, half)] + core_in[1, both(q)]
+            wide_x(q).start()
+
+        @pl.when(t == 2)
+        def _():
+            small_y.wait_recv()
+            t_ysum[...] = t_held[:, mine] + t_y[...]
+            small_x.start()
+
+        @pl.when((t >= 2) & (t < groups + 2))
+        def _():
+            q = near(t - 2)
+            along_y(q).wait_recv()
+            y_sum[both(q)] = held[0, both(q), mine] + y_in[both(q)]
+            along_x(q).start()
+            wide_x(q).wait_recv()
+            x_sum[q] = held[1, kept(q)] + x_wide[q]
+            late_y(q).start()
+
+        @pl.when(t == 4)
+        def _():
+            small_x.wait_recv()
+            t_xsum[...] = t_ysum[cut(parity, spread)] + t_x[...]
+
+            def send(p, inner):
+                small_z(peer(group, groups - p, groups)).start()
+                return inner
+
+            lax.fori_loop(1, groups, send, 0)
+
+        @pl.when((t >= 4) & (t < groups + 4))
+        def _():
+            q = near(t - 4)
+            along_x(q).wait_recv()
+            pair[q, rows:] = y_sum[kept(q)] + x_in[q]
+            late_y(q).wait_recv()
+            pair[q, :rows] = x_sum[q, :, mine] + y_late[q]
+
+            @pl.when(q != group)
+            def _():
+                along_z(q).start()
+
+        @pl.when(t == 6)
+        def _():
+            def take(p, total):
+                q = peer(group, p, groups)
+                remote(t_z.at[q], t_z.at[q], stz.at[q], rtz.at[q], {"mem": 2 * q + parity}).wait_recv()
+                return total + t_z[q]
+
+            final_s[...] = lax.fori_loop(1, groups, take, t_xsum[cut(group, extra)])
+            gather_s[slot] = final_s[...]
+
+            def send(p, inner):
+                small_gather(peer(me, members - p, members)).start()
+                return inner
+
+            lax.fori_loop(1, members, send, 0)
+
+        return carry
+
+    lax.fori_loop(0, max(groups, 4) + 4, step, 0)
+
+    def weights(at, who, where):
+        return remote(gather_w.at[at], gather_w.at[at], sgw.at[who], rgw.at[at], where)
+
+    def smalls(at, who, where):
+        return remote(gather_b.at[at], gather_b.at[at], sgb.at[who], rgb.at[at], where)
 
     far = (1 - high) * 2 + low
-    near = high * 2 + 1 - low
+    near_by = high * 2 + 1 - low
     near_far = (1 - high) * 2 + 1 - low
 
-    def send_small(p, carry):
-        small(peer(me, members - p, members)).start()
-        return carry
-
-    lax.fori_loop(1, members, send_small, 0)
-    weights(band, 0, across).start()
-    weights(band, 1, partner).start()
-
     def take_small(p, carry):
-        arrived(gather_s, r4, peer(me, p, members))
+        k = peer(me, p, members)
+        at = slot_of(k)
+        remote(gather_s.at[at], gather_s.at[at], stg.at[k], rtg.at[k], {"mem": k}).wait_recv()
         return carry
 
     lax.fori_loop(1, members, take_small, 0)
     gather_b[band] = gather_s[...]
     smalls(band, 0, across).start()
     smalls(band, 1, partner).start()
+
+    def take_z(p, total):
+        q = peer(group, groups - p, groups)
+        remote(z_in.at[q], z_in.at[q], sz.at[q], rz.at[q], {"mem": 2 * q + parity}).wait_recv()
+        return total + z_in[q]
+
+    gather_w[band] = lax.fori_loop(1, groups, take_z, pair[group])
+    weights(band, 0, across).start()
+    weights(band, 1, partner).start()
+    smalls(far, 2, across).wait_recv()
+    smalls(far, 2, partner).start()
     weights(far, 2, across).wait_recv()
     weights(far, 2, partner).start()
-    smalls(far, 2, across).wait_recv()
-    smalls(far, 2, partner).start()
-    for slot in (near, near_far):
-        weights(slot, 0, partner).wait_recv()
-        smalls(slot, 0, partner).wait_recv()
+    for at in (near_by, near_far):
+        smalls(at, 0, partner).wait_recv()
+        weights(at, 0, partner).wait_recv()
     for k in range(bands):
         lanes = slice((k % 2) * half + (k // 2) * part, (k % 2) * half + (k // 2) * part + part)
-        shares[:, lanes] = gather_w[k]
+        first_out[:, lanes] = gather_w[k, :rows]
+        second_out[:, lanes] = gather_w[k, rows:]
         small_all[:, lanes] = gather_b[k].reshape(small_all.shape[0], part)
-    for slot, who, where in ((band, 0, across), (band, 1, partner), (far, 2, partner)):
-        weights(slot, who, where).wait_send()
-        smalls(slot, who, where).wait_send()
+    for at, who, where in ((band, 0, across), (band, 1, partner), (far, 2, partner)):
+        weights(at, who, where).wait_send()
+        smalls(at, who, where).wait_send()
+    small_core.wait_send()
+    small_y.wait_send()
+    small_x.wait_send()
 
     def drain(k, carry):
-        one(k).wait_send()
-        two(k).wait_send()
-
         @pl.when(k != me)
         def _():
-            small(k).wait_send()
+            small_gather(k).wait_send()
 
         return carry
 
     def drain_groups(q, carry):
-        three(q).wait_send()
-
-        @pl.when(q != me // 2)
-        def _():
-            four(q).wait_send()
+        core(0, q).wait_send()
+        core(1, q).wait_send()
+        along_y(q).wait_send()
+        along_x(q).wait_send()
+        wide_x(q).wait_send()
+        late_y(q).wait_send()
+
+        @pl.when(q != group)
+        def _():
+            along_z(q).wait_send()
+            small_z(q).wait_send()
 
         return carry
 
     lax.fori_loop(0, members, drain, 0)
     lax.fori_loop(0, groups, drain_groups, 0)
+
+
+def reduce_scratch(members, bands, features, hidden, extra):
+    groups, rows, half, part = members // 2, features // members, hidden // 2, hidden // bands
+    dma = pltpu.SemaphoreType.DMA
+    height = members * extra
+    shapes = [
+        (2, features, half), (2, features, half), (features, part), (features, part),
+        (groups, rows, half), (groups, rows, half), (groups, rows, part), (groups, rows, part),
+        (groups, 2 * rows, part), (groups, 2 * rows, part), (bands, 2 * rows, part),
+        (height, half), (height, half), (height, part), (height, part),
+        (height // 2, part), (height // 2, part), (groups, extra, part),
+        (extra, part), (members, extra, part), (bands, members, extra, part),
+    ]
+    counts = (
+        [(2, groups)] * 2 + [(groups,)] * 10 + [(3,)] * 2 + [(groups,)] * 2 + [(members,)] * 2 + [(bands,)] * 4
+    )
+    return [pltpu.VMEM(o, jnp.float32) for o in shapes] + [dma(n) for n in counts]
 
 
 def score_kernel(
     members, bands, cols, edge,
     latent_ref, first_ref, first_bias_ref, second_ref, second_bias_ref, out_weight_ref, out_bias_ref,
-    truth_ref, node_ref,
+    truth_in, node_ref,
     score_out, first_out, first_bias_out, second_out, second_bias_out, out_weight_out, out_bias_out,
     rows_in, first_act, first_slope, second_act, second_slope, first_sum, second_sum, small_sum, bias_sum, raw_ref,
     before, after, grad_before, grad_after, sent, ensemble, grads, back,
     halo_send, halo_recv, fwd_send, fwd_recv, ret_send, ret_recv, ghalo_send, ghalo_recv, load,
-    score_ref, weight_ref, bias_column, g_ref, shares, small_all, *reduce_refs,
+    score_ref, weight_ref, bias_column, truth_ref, small_all, *reduce_refs,
 ):
     me = lax.axis_index("mem")
     band = lax.axis_index("band")
@@ -257,6 +354,7 @@
     shape = (channels, channels)
     diagonal = lax.broadcasted_iota(jnp.int32, shape, 0) == lax.broadcasted_iota(jnp.int32, shape, 1)
     bias_column[...] = jnp.sum(jnp.where(diagonal, out_bias_ref[...], 0.0), axis=1, keepdims=True)
+    truth_ref[...] = truth_in[...].reshape(length, channels).T
     for row in range(node_ref.shape[0]):
         weight_ref[:, row * cols : (row + 1) * cols] = node_ref[row : row + 1, :]
     pl.semaphore_wait(barrier, members + bands - 2)
@@ -440,14 +538,11 @@
     small_sum[channels + 2 : channels + 3, :channels] = jnp.sum(
         jnp.where(diagonal, bias_sum[...], 0.0), axis=0, keepdims=True
     )
-    g_ref[:, :rows] = first_sum[...].reshape(members, rows, hidden)
-    g_ref[:, rows : 2 * rows] = second_sum[...].reshape(members, rows, hidden)
-    g_ref[:, 2 * rows :] = small_sum[...].reshape(members, -1, hidden)
-    reduce_in_kernel(members, bands, rows, g_ref, shares, small_all, *reduce_refs)
+    reduce_in_kernel(
+        members, bands, first_sum, second_sum, small_sum, first_out, second_out, small_all, *reduce_refs
+    )
     for row in range(score_out.shape[0]):
         score_out[row : row + 1, :] = score_ref[:, row * cols : (row + 1) * cols]
-    first_out[...] = shares[:rows]
-    second_out[...] = shares[rows:]
     out_weight_out[...] = small_all[:channels]
     first_bias_out[...] = small_all[channels : channels + 1]
     second_bias_out[...] = small_all[channels + 1 : channels + 2]
@@ -469,10 +564,9 @@
 
 def score_and_gradient(latent, weights, truth, weight, members, bands, cols, rows, extra):
     lat_rows, _, features = latent.shape
-    channels, length = truth.shape
+    channels, length = truth.shape[2], lat_rows * cols
     hidden = weights[0].shape[1]
     edge = min(length, -(-RADIUS * cols // LANES) * LANES)
-    height, part = 2 * rows + extra, hidden // bands
     block = (members, channels, length)
     halo = (members, channels, edge)
     units = (members, length, hidden)
@@ -505,15 +599,9 @@
         + [dma((2, members))] * 2
         + [dma((members,))]
         + [pltpu.VMEM(o, single) for o in [
-            (1, length), (1, length), (channels, 1),
-            (members, height, hidden), (2 * rows, hidden), (members * extra, hidden),
-            (members, height, hidden // 2), (members, height, hidden // 2),
-            (members, height, part), (members, height, part),
-            (members // 2, height, part), (members // 2, height, part), (members // 2, height, part),
-            (extra, part), (bands, 2 * rows, part), (members, extra, part), (bands, members, extra, part),
+            (1, length), (1, length), (channels, 1), (channels, length), (members * extra, hidden),
         ]]
-        + [dma((n,)) for n in [members] * 4 + [members // 2] * 2 + [members] * 2]
-        + [dma((n,)) for n in [bands] * 4 + [members // 2] * 2],
+        + reduce_scratch(members, bands, features, hidden, extra),
         compiler_params=pltpu.CompilerParams(collective_id=0, has_side_effects=True, vmem_limit_bytes=60 << 20),
     )(latent, *weights, truth, weight)
 
@@ -548,7 +636,7 @@
     )
     score, first, first_b, second, second_b, out_w, out_b = write_results(score_and_gradient(
         latent.reshape(lat_rows, lon_cols, features), weights,
-        truth.reshape(channels, -1), node_weight, members, bands, cols, rows, extra,
+        jnp.transpose(truth, (1, 2, 0)), node_weight, members, bands, cols, rows, extra,
     ))
     return (score, first, first_b[0], second, second_b[0], out_w, out_b[0])
 

time: 118 us -> 109 us (0.924)
  Pallas kernels: 115 us -> 108 us
  local copies, waits for them, and re-layouts: 1.74 us -> 0 us
    pallas_call x1, Pallas kernels: 113 us -> 106 us  [score_and_gradient(): pl.pallas_call(functools.partial(score_kernel, members, bands, cols, edge...]
    reshape x1 -> x0, local copies, waits for them, and re-layouts: 1.74 us -> none  [body(): truth.reshape(channels, -1)]
where the time goes in v1:
time: 109 us; the launch traced here: 108 us
  Pallas kernels  108 us (99%)
    pallas_call x1, Pallas kernels, score_and_gradient(): pl.pallas_call(functools.partial(score_kernel, members, bands, cols, edge...  106 us

profile of v1, /device:TPU:0, one launch (start us, length us, event | category | flops | bytes accessed | tf_op | source)
XLA Modules:
  0.0 108.4 jit_solution(10124619227215575237)
XLA Ops:
  0.6 106.0 %shard_map.144 = (f32[8,64]{1,0:T(8,128)}, f32[64,512]{1,0:T(8,128)}, f32[1,512]{1,0:T(1,128)}, f32[64,512]{1,0:T(8,128)}, f32[1,512]{1,0:T(1,128)}, /*index=5*/f32[80,512]{1,0:T(8,128)}, f32[1,80]{1,0:T(1,128)}) custom-call(bf16[8,512,512]{2,1,0:T(8,128)(2,1)} %bitcast.8, bf16[512,512]{1,0:T(8,128)(2,1)} %first_ref.1, f32[1,512]{1,0:T(1,128)} %bitcast.10, ...), custom_call_target="tpu_custom_call" | custom-call | tf_op jit(solution)/shard_map/pallas_call | solution.py:576
  106.6 1.8 %shard_map.145 = (f32[8,64]{1,0:T(8,128)}, f32[64,512]{1,0:T(8,128)}, f32[1,512]{1,0:T(1,128)}, f32[64,512]{1,0:T(8,128)}, f32[1,512]{1,0:T(1,128)}, /*index=5*/f32[80,512]{1,0:T(8,128)}, f32[1,80]{1,0:T(1,128)}) custom-call(f32[8,64]{1,0:T(8,128)} %get-tuple-element.21.refs_0_, f32[64,512]{1,0:T(8,128)} %get-tuple-element.22.refs_1_, ...), custom_call_target="tpu_custom_call" | custom-call | tf_op jit(solution)/shard_map/pallas_call | solution.py:617

commit v2 on v1

--- a/solution.py
+++ b/solution.py
@@ -313,33 +313,45 @@
 
 
 def score_kernel(
-    members, bands, cols, edge,
+    members, bands, chunks, cols, edge,
     latent_ref, first_ref, first_bias_ref, second_ref, second_bias_ref, out_weight_ref, out_bias_ref,
     truth_in, node_ref,
     score_out, first_out, first_bias_out, second_out, second_bias_out, out_weight_out, out_bias_out,
     rows_in, first_act, first_slope, second_act, second_slope, first_sum, second_sum, small_sum, bias_sum, raw_ref,
-    before, after, grad_before, grad_after, sent, ensemble, grads, back,
-    halo_send, halo_recv, fwd_send, fwd_recv, ret_send, ret_recv, ghalo_send, ghalo_recv, load,
-    score_ref, weight_ref, bias_column, truth_ref, small_all, *reduce_refs,
+    before, after, grad_before, grad_after, sent, ensemble, grads, returned, back,
+    halo_send, halo_recv, ghalo_send, ghalo_recv, fwd_send, fwd_recv, ret_send, ret_recv, load,
+    score_ref, weight_ref, truth_ref, bias_column, small_all, *reduce_refs,
 ):
     me = lax.axis_index("mem")
     band = lax.axis_index("band")
     length = raw_ref.shape[2]
-    rows = first_out.shape[0]
+    lat_rows = node_ref.shape[0]
+    blocks = chunks * members
     taps = stencil_taps(RADIUS)
     has_prev = band > 0
     has_next = band < bands - 1
     prev, following = jnp.maximum(band - 1, 0), jnp.minimum(band + 1, bands - 1)
 
-    def fetch(k):
-        where = pl.ds(pl.multiple_of(k * cols, cols), cols)
-        return pltpu.make_async_copy(latent_ref.at[:, where, :], rows_in.at[k], load.at[k])
-
-    def prefetch(p, carry):
-        fetch(peer(me, members - p, members)).start()
-        return carry
-
-    lax.fori_loop(1, members + 1, prefetch, 0)
+    def outward(s):
+        return peer(me, members - 1 - lax.rem(s, members), members)
+
+    def inward(s):
+        return peer(me, lax.rem(s, members), members)
+
+    def block_of(s, k):
+        return (s // members) * members + k
+
+    def fetch(s):
+        chunk, k = s // members, outward(s)
+        where = pl.ds(pl.multiple_of((k * chunks + chunk) * cols, cols), cols)
+        b = block_of(s, k)
+        return pltpu.make_async_copy(latent_ref.at[:, where, :], rows_in.at[b], load.at[b])
+
+    def prefetch(s, carry):
+        fetch(s).start()
+        return carry
+
+    lax.fori_loop(0, blocks, prefetch, 0)
     barrier = pltpu.get_barrier_semaphore()
 
     def greet(p, carry):
@@ -354,10 +366,10 @@
     shape = (channels, channels)
     diagonal = lax.broadcasted_iota(jnp.int32, shape, 0) == lax.broadcasted_iota(jnp.int32, shape, 1)
     bias_column[...] = jnp.sum(jnp.where(diagonal, out_bias_ref[...], 0.0), axis=1, keepdims=True)
-    truth_ref[...] = truth_in[...].reshape(length, channels).T
-    for row in range(node_ref.shape[0]):
-        weight_ref[:, row * cols : (row + 1) * cols] = node_ref[row : row + 1, :]
-    pl.semaphore_wait(barrier, members + bands - 2)
+    for c in range(chunks):
+        truth_ref[c] = truth_in[:, c * cols : (c + 1) * cols, :].reshape(length, channels).T
+        for row in range(lat_rows):
+            weight_ref[c, :, row * cols : (row + 1) * cols] = node_ref[row : row + 1, c * cols : (c + 1) * cols]
 
     @pl.when(band == 0)
     def _():
@@ -369,212 +381,234 @@
         after[...] = jnp.zeros_like(after)
         grad_after[...] = jnp.zeros_like(grad_after)
 
-    def to_next(source, target, k, send, recv):
-        return remote(source.at[k, :, pl.ds(length - edge, edge)], target.at[k], send.at[0, k], recv.at[0, k], {"band": following})
-
-    def to_prev(source, target, k, send, recv):
-        return remote(source.at[k, :, pl.ds(0, edge)], target.at[k], send.at[1, k], recv.at[1, k], {"band": prev})
-
-    def start_edges(source, low, high, k, send, recv):
+    pl.semaphore_wait(barrier, members + bands - 2)
+
+    def to_next(source, target, b, send, recv):
+        return remote(source.at[b, :, pl.ds(length - edge, edge)], target.at[b], send.at[0, b], recv.at[0, b], {"band": following})
+
+    def to_prev(source, target, b, send, recv):
+        return remote(source.at[b, :, pl.ds(0, edge)], target.at[b], send.at[1, b], recv.at[1, b], {"band": prev})
+
+    def start_edges(source, low, high, b, send, recv):
         @pl.when(has_next)
         def _():
-            to_next(source, low, k, send, recv).start()
+            to_next(source, low, b, send, recv).start()
 
         @pl.when(has_prev)
         def _():
-            to_prev(source, high, k, send, recv).start()
-
-    def wait_edges(source, low, high, k, send, recv):
+            to_prev(source, high, b, send, recv).start()
+
+    def wait_edges(source, low, high, b, send, recv):
         @pl.when(has_prev)
         def _():
-            to_next(source, low, k, send, recv).wait_recv()
+            to_next(source, low, b, send, recv).wait_recv()
 
         @pl.when(has_next)
         def _():
-            to_prev(source, high, k, send, recv).wait_recv()
-
-    def drain_edges(source, low, high, k, send, recv):
+            to_prev(source, high, b, send, recv).wait_recv()
+
+    def drain_edges(source, low, high, b, send, recv):
         @pl.when(has_next)
         def _():
-            to_next(source, low, k, send, recv).wait_send()
+            to_next(source, low, b, send, recv).wait_send()
 
         @pl.when(has_prev)
         def _():
-            to_prev(source, high, k, send, recv).wait_send()
+            to_prev(source, high, b, send, recv).wait_send()
 
     raw_edges = (raw_ref, before, after)
-    grad_edges = (back, grad_before, grad_after)
-
-    def forward(k):
-        return remote(sent.at[k], ensemble.at[me], fwd_send.at[k], fwd_recv.at[me], {"mem": k})
-
-    def returning(k):
-        return remote(grads.at[k], back.at[me], ret_send.at[k], ret_recv.at[me], {"mem": k})
-
-    def arrived(buffer, sems, k):
-        remote(buffer.at[k], buffer.at[k], sems.at[k], sems.at[k], {"mem": k}).wait_recv()
-
-    def decode(k):
-        fetch(k).wait()
-        inputs = rows_in[k].reshape(length, rows_in.shape[3])
+    grad_edges = (grads, grad_before, grad_after)
+
+    def forward(s, k):
+        b = block_of(s, k)
+        return remote(sent.at[b], ensemble.at[block_of(s, me)], fwd_send.at[b], fwd_recv.at[block_of(s, me)], {"mem": k})
+
+    def returning(s, k):
+        b = block_of(s, k)
+        return remote(returned.at[b], back.at[block_of(s, me)], ret_send.at[b], ret_recv.at[block_of(s, me)], {"mem": k})
+
+    def arrived(buffer, sems, s, k):
+        b = block_of(s, k)
+        remote(buffer.at[b], buffer.at[b], sems.at[b], sems.at[b], {"mem": k}).wait_recv()
+
+    def decode(s):
+        b = block_of(s, outward(s))
+        fetch(s).wait()
+        inputs = rows_in[b].reshape(length, rows_in.shape[3])
         pre = jnp.dot(inputs, first_ref[...], preferred_element_type=jnp.float32) + first_bias_ref[...]
         act, slope = gelu_pair(pre)
-        first_act[k] = act.astype(jnp.bfloat16)
-        first_slope[k] = slope
-        pre = jnp.dot(first_act[k], second_ref[...], preferred_element_type=jnp.float32) + second_bias_ref[...]
+        first_act[b] = act.astype(jnp.bfloat16)
+        first_slope[b] = slope
+        pre = jnp.dot(first_act[b], second_ref[...], preferred_element_type=jnp.float32) + second_bias_ref[...]
         act, slope = gelu_pair(pre)
-        second_act[k] = act.astype(jnp.bfloat16)
-        second_slope[k] = slope
-        raw_ref[k] = contract(out_weight_ref[...], second_act[k], 1, 1) + bias_column[...]
-
-    def spread(p):
-        k = peer(me, members - p, members)
-        wait_edges(*raw_edges, k, halo_send, halo_recv)
-        smooth = smooth_block(before[k], raw_ref[k], after[k], taps, cols)
-
-        @pl.when(p < members)
-        def _():
-            sent[k] = smooth
-            forward(k).start()
-
-        @pl.when(p == members)
-        def _():
-            ensemble[k] = smooth
-
-    def forward_step(p, carry):
-        @pl.when(p <= members)
-        def _():
-            k = peer(me, members - p, members)
-            decode(k)
-            start_edges(*raw_edges, k, halo_send, halo_recv)
-
-        @pl.when(p >= 2)
-        def _():
-            spread(p - 1)
-
-        return carry
-
-    lax.fori_loop(1, members + 2, forward_step, 0)
-
-    def collect(p, carry):
-        arrived(ensemble, fwd_recv, peer(me, p, members))
-        return carry
-
-    lax.fori_loop(1, members, collect, 0)
-    score_ref[...] = jnp.zeros_like(score_ref)
-    pair_count = members * (members - 1)
-    row_ids = lax.broadcasted_iota(jnp.int32, (members, LANES), 0)
-
-    def member(p, carry):
-        m = peer(me, members - p, members)
-
-        def chunk(c, inner):
-            lanes = pl.ds(pl.multiple_of(c * LANES, LANES), LANES)
-            mine = ensemble[m, :, lanes]
-            gaps = mine[None] - ensemble[:, :, lanes]
-            distance = jnp.sqrt(jnp.sum(gaps * gaps, axis=1) + epsilon)
-            own = row_ids == m
-            inverse = jnp.where(own, 0.0, 1.0 / distance)
-            spread_sum = jnp.sum(jnp.where(own, 0.0, distance), axis=0, keepdims=True)
-            pair_grad = jnp.sum(gaps * inverse[:, None, :], axis=0)
-            error = mine - truth_ref[:, lanes]
-            skill = jnp.sqrt(jnp.sum(error * error, axis=0, keepdims=True) + epsilon)
-            score_ref[:, lanes] += skill / members - spread_sum / (2.0 * pair_count)
-            result = weight_ref[:, lanes] * (error / (members * skill) - pair_grad / pair_count)
-
-            @pl.when(p < members)
-            def _():
-                grads[m, :, lanes] = result
-
-            @pl.when(p == members)
-            def _():
-                back[m, :, lanes] = result
-
-            return inner
-
-        lax.fori_loop(0, length // LANES, chunk, 0)
-
-        @pl.when(p < members)
-        def _():
-            returning(m).start()
-
-        return carry
-
-    lax.fori_loop(1, members + 1, member, 0)
-    start_edges(*grad_edges, me, ghalo_send, ghalo_recv)
-
+        second_act[b] = act.astype(jnp.bfloat16)
+        second_slope[b] = slope
+        raw_ref[b] = contract(out_weight_ref[...], second_act[b], 1, 1) + bias_column[...]
+        start_edges(*raw_edges, b, halo_send, halo_recv)
+
+    def spread(s):
+        k = outward(s)
+        b = block_of(s, k)
+        wait_edges(*raw_edges, b, halo_send, halo_recv)
+        smooth = smooth_block(before[b], raw_ref[b], after[b], taps, cols)
+
+        @pl.when(k != me)
+        def _():
+            sent[b] = smooth
+            forward(s, k).start()
+
+        @pl.when(k == me)
+        def _():
+            ensemble[b] = smooth
+
+    lag = 2
+
+    def forward_step(s, carry):
+        @pl.when(s < blocks)
+        def _():
+            decode(s)
+
+        @pl.when(s >= lag)
+        def _():
+            spread(s - lag)
+
+        return carry
+
+    lax.fori_loop(0, blocks + lag, forward_step, 0)
     first_sum[...] = jnp.zeros_like(first_sum)
     second_sum[...] = jnp.zeros_like(second_sum)
     small_sum[...] = jnp.zeros_like(small_sum)
     bias_sum[...] = jnp.zeros_like(bias_sum)
-
-    def finish(p):
-        k = peer(me, p, members)
-        wait_edges(*grad_edges, k, ghalo_send, ghalo_recv)
-        grad_raw = smooth_block(grad_before[k], back[k], grad_after[k], taps, cols)
+    score_ref[...] = jnp.zeros_like(score_ref)
+    pair_count = members * (members - 1)
+    row_ids = lax.broadcasted_iota(jnp.int32, (members, LANES), 0)
+
+    def score_chunk(c, carry):
+        start = c * members
+
+        def collect(p, inner):
+            arrived(ensemble, fwd_recv, start, peer(me, p, members))
+            return inner
+
+        lax.fori_loop(1, members, collect, 0)
+
+        def member(p, inner):
+            m = outward(p)
+            b = start + m
+
+            def piece(i, innermost):
+                lanes = pl.ds(pl.multiple_of(i * LANES, LANES), LANES)
+                mine = ensemble[b, :, lanes]
+                gaps = mine[None] - ensemble[pl.ds(start, members), :, lanes]
+                distance = jnp.sqrt(jnp.sum(gaps * gaps, axis=1) + epsilon)
+                own = row_ids == m
+                inverse = jnp.where(own, 0.0, 1.0 / distance)
+                spread_sum = jnp.sum(jnp.where(own, 0.0, distance), axis=0, keepdims=True)
+                pair_grad = jnp.sum(gaps * inverse[:, None, :], axis=0)
+                error = mine - truth_ref[c, :, lanes]
+                skill = jnp.sqrt(jnp.sum(error * error, axis=0, keepdims=True) + epsilon)
+                score_ref[c, :, lanes] += skill / members - spread_sum / (2.0 * pair_count)
+                grads[b, :, lanes] = weight_ref[c, :, lanes] * (error / (members * skill) - pair_grad / pair_count)
+                return innermost
+
+            lax.fori_loop(0, length // LANES, piece, 0)
+            start_edges(*grad_edges, b, ghalo_send, ghalo_recv)
+            return inner
+
+        lax.fori_loop(0, members, member, 0)
+
+        def give(p, inner):
+            m = outward(p)
+            b = start + m
+            wait_edges(*grad_edges, b, ghalo_send, ghalo_recv)
+            smooth = smooth_block(grad_before[b], grads[b], grad_after[b], taps, cols)
+
+            @pl.when(m != me)
+            def _():
+                returned[b] = smooth
+                returning(start, m).start()
+
+            @pl.when(m == me)
+            def _():
+                back[b] = smooth
+
+            return inner
+
+        lax.fori_loop(0, members, give, 0)
+        return carry
+
+    lax.fori_loop(0, chunks, score_chunk, 0)
+
+    def finish(s, carry):
+        k = inward(s)
+        b = block_of(s, k)
+
+        @pl.when(k != me)
+        def _():
+            arrived(back, ret_recv, s, k)
+
+        grad_raw = back[b]
         grad_low = grad_raw.astype(jnp.bfloat16)
         bias_sum[...] += jnp.sum(grad_raw, axis=1, keepdims=True)
-        small_sum[:channels] += jnp.dot(grad_low, second_act[k], preferred_element_type=jnp.float32)
-        delta = contract(grad_low, out_weight_ref[...], 0, 0) * second_slope[k]
+        small_sum[:channels] += jnp.dot(grad_low, second_act[b], preferred_element_type=jnp.float32)
+        delta = contract(grad_low, out_weight_ref[...], 0, 0) * second_slope[b]
         small_sum[channels + 1 : channels + 2] += jnp.sum(delta, axis=0, keepdims=True)
         low = delta.astype(jnp.bfloat16)
-        second_sum[...] += contract(first_act[k], low, 0, 0)
-        delta = contract(low, second_ref[...], 1, 1) * first_slope[k]
+        second_sum[...] += contract(first_act[b], low, 0, 0)
+        delta = contract(low, second_ref[...], 1, 1) * first_slope[b]
         small_sum[channels : channels + 1] += jnp.sum(delta, axis=0, keepdims=True)
-        inputs = rows_in[k].reshape(length, rows_in.shape[3])
+        inputs = rows_in[b].reshape(length, rows_in.shape[3])
         first_sum[...] += contract(inputs, delta.astype(jnp.bfloat16), 0, 0)
-
-    def backward_step(p, carry):
-        @pl.when(p < members)
-        def _():
-            k = peer(me, p, members)
-            arrived(back, ret_recv, k)
-            start_edges(*grad_edges, k, ghalo_send, ghalo_recv)
-
-        finish(p - 1)
-        return carry
-
-    lax.fori_loop(1, members + 1, backward_step, 0)
+        return carry
+
+    lax.fori_loop(0, blocks, finish, 0)
     small_sum[channels + 2 : channels + 3, :channels] = jnp.sum(
         jnp.where(diagonal, bias_sum[...], 0.0), axis=0, keepdims=True
     )
     reduce_in_kernel(
         members, bands, first_sum, second_sum, small_sum, first_out, second_out, small_all, *reduce_refs
     )
-    for row in range(score_out.shape[0]):
-        score_out[row : row + 1, :] = score_ref[:, row * cols : (row + 1) * cols]
+    for c in range(chunks):
+        for row in range(lat_rows):
+            score_out[row : row + 1, c * cols : (c + 1) * cols] = score_ref[c, :, row * cols : (row + 1) * cols]
     out_weight_out[...] = small_all[:channels]
     first_bias_out[...] = small_all[channels : channels + 1]
     second_bias_out[...] = small_all[channels + 1 : channels + 2]
     out_bias_out[...] = small_all[channels + 2 : channels + 3, :channels]
 
-    def drain(k, carry):
-        drain_edges(*raw_edges, k, halo_send, halo_recv)
-        drain_edges(*grad_edges, k, ghalo_send, ghalo_recv)
+    def drain(s, carry):
+        k = inward(s)
+        b = block_of(s, k)
+        drain_edges(*raw_edges, b, halo_send, halo_recv)
+        drain_edges(*grad_edges, b, ghalo_send, ghalo_recv)
 
         @pl.when(k != me)
         def _():
-            forward(k).wait_send()
-            returning(k).wait_send()
-
-        return carry
-
-    lax.fori_loop(0, members, drain, 0)
+            forward(s, k).wait_send()
+            returning(s, k).wait_send()
+
+        return carry
+
+    lax.fori_loop(0, blocks, drain, 0)
 
 
 def score_and_gradient(latent, weights, truth, weight, members, bands, cols, rows, extra):
     lat_rows, _, features = latent.shape
-    channels, length = truth.shape[2], lat_rows * cols
+    channels = truth.shape[2]
     hidden = weights[0].shape[1]
-    edge = min(length, -(-RADIUS * cols // LANES) * LANES)
-    block = (members, channels, length)
-    halo = (members, channels, edge)
-    units = (members, length, hidden)
+    chunks = 2 if cols % 32 == 0 and lat_rows * cols % (2 * LANES) == 0 else 1
+    part_cols = cols // chunks
+    length = lat_rows * part_cols
+    edge = min(length, -(-RADIUS * part_cols // LANES) * LANES)
+    blocks = chunks * members
+    block = (blocks, channels, length)
+    halo = (blocks, channels, edge)
+    units = (blocks, length, hidden)
     dma = pltpu.SemaphoreType.DMA
     vmem = pl.BlockSpec(memory_space=pltpu.VMEM)
     single, half = jnp.float32, jnp.bfloat16
     return pl.pallas_call(
-        functools.partial(score_kernel, members, bands, cols, edge),
+        functools.partial(score_kernel, members, bands, chunks, part_cols, edge),
         out_shape=tuple(
             jax.ShapeDtypeStruct(o, single)
             for o in (
@@ -585,7 +619,7 @@
         in_specs=[pl.BlockSpec(memory_space=pl.ANY)] + [vmem] * 8,
         out_specs=(vmem,) * 7,
         scratch_shapes=[
-            pltpu.VMEM((members, lat_rows, cols, features), half),
+            pltpu.VMEM((blocks, lat_rows, part_cols, features), half),
             pltpu.VMEM(units, half), pltpu.VMEM(units, single),
             pltpu.VMEM(units, half), pltpu.VMEM(units, single),
             pltpu.VMEM((features, hidden), single), pltpu.VMEM((hidden, hidden), single),
@@ -593,13 +627,12 @@
             pltpu.VMEM(block, single),
         ]
         + [pltpu.VMEM(halo, single)] * 4
-        + [pltpu.VMEM(block, single)] * 4
-        + [dma((2, members))] * 2
-        + [dma((members,))] * 4
-        + [dma((2, members))] * 2
-        + [dma((members,))]
+        + [pltpu.VMEM(block, single)] * 5
+        + [dma((2, blocks))] * 4
+        + [dma((blocks,))] * 5
         + [pltpu.VMEM(o, single) for o in [
-            (1, length), (1, length), (channels, 1), (channels, length), (members * extra, hidden),
+            (chunks, 1, length), (chunks, 1, length), (chunks, channels, length), (channels, 1),
+            (members * extra, hidden),
         ]]
         + reduce_scratch(members, bands, features, hidden, extra),
         compiler_params=pltpu.CompilerParams(collective_id=0, has_side_effects=True, vmem_limit_bytes=60 << 20),

time: 109 us -> 104 us (0.954)
  Pallas kernels: 108 us -> 103 us
    pallas_call x1, Pallas kernels: 106 us -> 101 us  [score_and_gradient(): pl.pallas_call(functools.partial(score_kernel, members, bands, chunks, pa...]
where the time goes in v2:
time: 104 us
  Pallas kernels  103 us (99%)
    pallas_call x1, Pallas kernels, score_and_gradient(): pl.pallas_call(functools.partial(score_kernel, members, bands, chunks, pa...  101 us

profile of v2, /device:TPU:0, one launch (start us, length us, event | category | flops | bytes accessed | tf_op | source)
XLA Modules:
  0.0 103.6 jit_solution(16849422084391588826)
XLA Ops:
  0.6 101.1 %shard_map.144 = (f32[8,64]{1,0:T(8,128)}, f32[64,512]{1,0:T(8,128)}, f32[1,512]{1,0:T(1,128)}, f32[64,512]{1,0:T(8,128)}, f32[1,512]{1,0:T(1,128)}, /*index=5*/f32[80,512]{1,0:T(8,128)}, f32[1,80]{1,0:T(1,128)}) custom-call(bf16[8,512,512]{2,1,0:T(8,128)(2,1)} %bitcast.8, bf16[512,512]{1,0:T(8,128)(2,1)} %first_ref.1, f32[1,512]{1,0:T(1,128)} %bitcast.10, ...), custom_call_target="tpu_custom_call" | custom-call | tf_op jit(solution)/shard_map/pallas_call | solution.py:610
  101.7 1.8 %shard_map.145 = (f32[8,64]{1,0:T(8,128)}, f32[64,512]{1,0:T(8,128)}, f32[1,512]{1,0:T(1,128)}, f32[64,512]{1,0:T(8,128)}, f32[1,512]{1,0:T(1,128)}, /*index=5*/f32[80,512]{1,0:T(8,128)}, f32[1,80]{1,0:T(1,128)}) custom-call(f32[8,64]{1,0:T(8,128)} %get-tuple-element.21.refs_0_, f32[64,512]{1,0:T(8,128)} %get-tuple-element.22.refs_1_, ...), custom_call_target="tpu_custom_call" | custom-call | tf_op jit(solution)/shard_map/pallas_call | solution.py:650

commit v3 on v2

--- a/solution.py
+++ b/solution.py
@@ -314,9 +314,10 @@
 
 def score_kernel(
     members, bands, chunks, cols, edge,
-    latent_ref, first_ref, first_bias_ref, second_ref, second_bias_ref, out_weight_ref, out_bias_ref,
-    truth_in, node_ref,
+    latent_ref, first_hbm, first_bias_hbm, second_hbm, second_bias_hbm, out_weight_hbm, out_bias_hbm,
+    truth_hbm, node_hbm,
     score_out, first_out, first_bias_out, second_out, second_bias_out, out_weight_out, out_bias_out,
+    first_ref, first_bias_ref, second_ref, second_bias_ref, out_weight_ref, out_bias_ref, truth_in, node_ref, inputs_sem,
     rows_in, first_act, first_slope, second_act, second_slope, first_sum, second_sum, small_sum, bias_sum, raw_ref,
     before, after, grad_before, grad_after, sent, ensemble, grads, returned, back,
     halo_send, halo_recv, ghalo_send, ghalo_recv, fwd_send, fwd_recv, ret_send, ret_recv, load,
@@ -351,7 +352,6 @@
         fetch(s).start()
         return carry
 
-    lax.fori_loop(0, blocks, prefetch, 0)
     barrier = pltpu.get_barrier_semaphore()
 
     def greet(p, carry):
@@ -362,15 +362,22 @@
 
     for d in range(1, bands):
         pl.semaphore_signal(barrier, inc=1, device_id={"band": lax.rem(band + d, bands)}, device_id_type=MESH)
+
+    pairs = (
+        (first_hbm, first_ref), (first_bias_hbm, first_bias_ref), (second_hbm, second_ref),
+        (second_bias_hbm, second_bias_ref), (out_weight_hbm, out_weight_ref), (out_bias_hbm, out_bias_ref),
+        (truth_hbm, truth_in), (node_hbm, node_ref),
+    )
+    loads = [pltpu.make_async_copy(source, target, inputs_sem.at[i]) for i, (source, target) in enumerate(pairs)]
+    for copy in loads[:2]:
+        copy.start()
+    fetch(0).start()
+    for copy in loads[2:6]:
+        copy.start()
+    lax.fori_loop(1, blocks, prefetch, 0)
+    for copy in loads[6:]:
+        copy.start()
     channels, hidden = out_weight_ref.shape
-    shape = (channels, channels)
-    diagonal = lax.broadcasted_iota(jnp.int32, shape, 0) == lax.broadcasted_iota(jnp.int32, shape, 1)
-    bias_column[...] = jnp.sum(jnp.where(diagonal, out_bias_ref[...], 0.0), axis=1, keepdims=True)
-    for c in range(chunks):
-        truth_ref[c] = truth_in[:, c * cols : (c + 1) * cols, :].reshape(length, channels).T
-        for row in range(lat_rows):
-            weight_ref[c, :, row * cols : (row + 1) * cols] = node_ref[row : row + 1, c * cols : (c + 1) * cols]
-
     @pl.when(band == 0)
     def _():
         before[...] = jnp.zeros_like(before)
@@ -380,8 +387,6 @@
     def _():
         after[...] = jnp.zeros_like(after)
         grad_after[...] = jnp.zeros_like(grad_after)
-
-    pl.semaphore_wait(barrier, members + bands - 2)
 
     def to_next(source, target, b, send, recv):
         return remote(source.at[b, :, pl.ds(length - edge, edge)], target.at[b], send.at[0, b], recv.at[0, b], {"band": following})
@@ -444,7 +449,9 @@
         second_act[b] = act.astype(jnp.bfloat16)
         second_slope[b] = slope
         raw_ref[b] = contract(out_weight_ref[...], second_act[b], 1, 1) + bias_column[...]
-        start_edges(*raw_edges, b, halo_send, halo_recv)
+
+    def decode_edges(s):
+        start_edges(*raw_edges, block_of(s, outward(s)), halo_send, halo_recv)
 
     def spread(s):
         k = outward(s)
@@ -461,20 +468,40 @@
         def _():
             ensemble[b] = smooth
 
-    lag = 2
+    lead = 2
+
+    def early_step(s, carry):
+        decode(s)
+        return carry
+
+    def early_edges(s, carry):
+        decode_edges(s)
+        return carry
 
     def forward_step(s, carry):
         @pl.when(s < blocks)
         def _():
             decode(s)
-
-        @pl.when(s >= lag)
-        def _():
-            spread(s - lag)
-
-        return carry
-
-    lax.fori_loop(0, blocks + lag, forward_step, 0)
+            decode_edges(s)
+
+        spread(s - lead)
+        return carry
+
+    for copy in loads[:6]:
+        copy.wait()
+    shape = (channels, channels)
+    diagonal = lax.broadcasted_iota(jnp.int32, shape, 0) == lax.broadcasted_iota(jnp.int32, shape, 1)
+    bias_column[...] = jnp.sum(jnp.where(diagonal, out_bias_ref[...], 0.0), axis=1, keepdims=True)
+    lax.fori_loop(0, lead, early_step, 0)
+    pl.semaphore_wait(barrier, members + bands - 2)
+    lax.fori_loop(0, lead, early_edges, 0)
+    lax.fori_loop(lead, blocks + lead, forward_step, 0)
+    for copy in loads[6:]:
+        copy.wait()
+    for c in range(chunks):
+        truth_ref[c] = truth_in[:, c * cols : (c + 1) * cols, :].reshape(length, channels).T
+        for row in range(lat_rows):
+            weight_ref[c, :, row * cols : (row + 1) * cols] = node_ref[row : row + 1, c * cols : (c + 1) * cols]
     first_sum[...] = jnp.zeros_like(first_sum)
     second_sum[...] = jnp.zeros_like(second_sum)
     small_sum[...] = jnp.zeros_like(small_sum)
@@ -616,9 +643,11 @@
                 (channels, hidden), (1, channels),
             )
         ),
-        in_specs=[pl.BlockSpec(memory_space=pl.ANY)] + [vmem] * 8,
+        in_specs=[pl.BlockSpec(memory_space=pl.ANY)] * 9,
         out_specs=(vmem,) * 7,
-        scratch_shapes=[
+        scratch_shapes=[pltpu.VMEM(v.shape, v.dtype) for v in (*weights, truth, weight)]
+        + [dma((8,))]
+        + [
             pltpu.VMEM((blocks, lat_rows, part_cols, features), half),
             pltpu.VMEM(units, half), pltpu.VMEM(units, single),
             pltpu.VMEM(units, half), pltpu.VMEM(units, single),

time: 104 us -> 101 us (0.971)
  Pallas kernels: 103 us -> 100 us
    pallas_call x1, Pallas kernels: 101 us -> 98.1 us  [score_and_gradient(): pl.pallas_call(functools.partial(score_kernel, members, bands, chunks, pa...]
where the time goes in v3:
time: 101 us
  Pallas kernels  100 us (99%)
    pallas_call x1, Pallas kernels, score_and_gradient(): pl.pallas_call(functools.partial(score_kernel, members, bands, chunks, pa...  98.1 us

profile of v3, /device:TPU:0, one launch (start us, length us, event | category | flops | bytes accessed | tf_op | source)
XLA Modules:
  0.0 100.6 jit_solution(17393353975629848490)
XLA Ops:
  0.6 98.1 %shard_map.144 = (f32[8,64]{1,0:T(8,128)}, f32[64,512]{1,0:T(8,128)}, f32[1,512]{1,0:T(1,128)}, f32[64,512]{1,0:T(8,128)}, f32[1,512]{1,0:T(1,128)}, /*index=5*/f32[80,512]{1,0:T(8,128)}, f32[1,80]{1,0:T(1,128)}) custom-call(bf16[8,512,512]{2,1,0:T(8,128)(2,1)} %bitcast.8, bf16[512,512]{1,0:T(8,128)(2,1)} %first_hbm.1, f32[1,512]{1,0:T(1,128)} %bitcast.10, ...), custom_call_target="tpu_custom_call" | custom-call | tf_op jit(solution)/shard_map/pallas_call | solution.py:637
  98.8 1.8 %shard_map.145 = (f32[8,64]{1,0:T(8,128)}, f32[64,512]{1,0:T(8,128)}, f32[1,512]{1,0:T(1,128)}, f32[64,512]{1,0:T(8,128)}, f32[1,512]{1,0:T(1,128)}, /*index=5*/f32[80,512]{1,0:T(8,128)}, f32[1,80]{1,0:T(1,128)}) custom-call(f32[8,64]{1,0:T(8,128)} %get-tuple-element.21.refs_0_, f32[64,512]{1,0:T(8,128)} %get-tuple-element.22.refs_1_, ...), custom_call_target="tpu_custom_call" | custom-call | tf_op jit(solution)/shard_map/pallas_call | solution.py:679

commit v4 on v3

--- a/solution.py
+++ b/solution.py
@@ -334,10 +334,12 @@
     prev, following = jnp.maximum(band - 1, 0), jnp.minimum(band + 1, bands - 1)
 
     def outward(s):
-        return peer(me, members - 1 - lax.rem(s, members), members)
+        p = lax.rem(s, members)
+        far = members - 1 - p // 2
+        return peer(me, jnp.where(lax.rem(p, 2) == 0, far, far - members // 2), members)
 
     def inward(s):
-        return peer(me, lax.rem(s, members), members)
+        return outward(lax.rem(s, members) + members - 1)
 
     def block_of(s, k):
         return (s // members) * members + k

time: 101 us -> 99.4 us (0.984)
  Pallas kernels: 100 us -> 98.6 us
    pallas_call x1, Pallas kernels: 98.1 us -> 96.8 us  [score_and_gradient(): pl.pallas_call(functools.partial(score_kernel, members, bands, chunks, pa...]
where the time goes in v4:
time: 99.4 us; the launch traced here: 99.3 us
  Pallas kernels  98.6 us (99%)
    pallas_call x1, Pallas kernels, score_and_gradient(): pl.pallas_call(functools.partial(score_kernel, members, bands, chunks, pa...  96.8 us

profile of v4, /device:TPU:0, one launch (start us, length us, event | category | flops | bytes accessed | tf_op | source)
XLA Modules:
  0.0 99.3 jit_solution(1202117067048231969)
XLA Ops:
  0.6 96.8 %shard_map.144 = (f32[8,64]{1,0:T(8,128)}, f32[64,512]{1,0:T(8,128)}, f32[1,512]{1,0:T(1,128)}, f32[64,512]{1,0:T(8,128)}, f32[1,512]{1,0:T(1,128)}, /*index=5*/f32[80,512]{1,0:T(8,128)}, f32[1,80]{1,0:T(1,128)}) custom-call(bf16[8,512,512]{2,1,0:T(8,128)(2,1)} %bitcast.8, bf16[512,512]{1,0:T(8,128)(2,1)} %first_hbm.1, f32[1,512]{1,0:T(1,128)} %bitcast.10, ...), custom_call_target="tpu_custom_call" | custom-call | tf_op jit(solution)/shard_map/pallas_call | solution.py:639
  97.4 1.8 %shard_map.145 = (f32[8,64]{1,0:T(8,128)}, f32[64,512]{1,0:T(8,128)}, f32[1,512]{1,0:T(1,128)}, f32[64,512]{1,0:T(8,128)}, f32[1,512]{1,0:T(1,128)}, /*index=5*/f32[80,512]{1,0:T(8,128)}, f32[1,80]{1,0:T(1,128)}) custom-call(f32[8,64]{1,0:T(8,128)} %get-tuple-element.21.refs_0_, f32[64,512]{1,0:T(8,128)} %get-tuple-element.22.refs_1_, ...), custom_call_target="tpu_custom_call" | custom-call | tf_op jit(solution)/shard_map/pallas_call | solution.py:681

commit v5 on v4

--- a/solution.py
+++ b/solution.py
@@ -177,7 +177,7 @@
             x_sum[q] = held[1, kept(q)] + x_wide[q]
             late_y(q).start()
 
-        @pl.when(t == 4)
+        @pl.when(t == 3)
         def _():
             small_x.wait_recv()
             t_xsum[...] = t_ysum[cut(parity, spread)] + t_x[...]
@@ -200,7 +200,7 @@
             def _():
                 along_z(q).start()
 
-        @pl.when(t == 6)
+        @pl.when(t == 4)
         def _():
             def take(p, total):
                 q = peer(group, p, groups)

time: 99.4 us -> 98.1 us (0.987)
  Pallas kernels: 98.6 us -> 97.3 us
    pallas_call x1, Pallas kernels: 96.8 us -> 95.5 us  [score_and_gradient(): pl.pallas_call(functools.partial(score_kernel, members, bands, chunks, pa...]
where the time goes in v5:
time: 98.1 us; the launch traced here: 97.9 us
  Pallas kernels  97.3 us (99%)
    pallas_call x1, Pallas kernels, score_and_gradient(): pl.pallas_call(functools.partial(score_kernel, members, bands, chunks, pa...  95.5 us

profile of v5, /device:TPU:0, one launch (start us, length us, event | category | flops | bytes accessed | tf_op | source)
XLA Modules:
  0.0 97.9 jit_solution(13096711706218595041)
XLA Ops:
  0.6 95.5 %shard_map.144 = (f32[8,64]{1,0:T(8,128)}, f32[64,512]{1,0:T(8,128)}, f32[1,512]{1,0:T(1,128)}, f32[64,512]{1,0:T(8,128)}, f32[1,512]{1,0:T(1,128)}, /*index=5*/f32[80,512]{1,0:T(8,128)}, f32[1,80]{1,0:T(1,128)}) custom-call(bf16[8,512,512]{2,1,0:T(8,128)(2,1)} %bitcast.8, bf16[512,512]{1,0:T(8,128)(2,1)} %first_hbm.1, f32[1,512]{1,0:T(1,128)} %bitcast.10, ...), custom_call_target="tpu_custom_call" | custom-call | tf_op jit(solution)/shard_map/pallas_call | solution.py:639
  96.1 1.8 %shard_map.145 = (f32[8,64]{1,0:T(8,128)}, f32[64,512]{1,0:T(8,128)}, f32[1,512]{1,0:T(1,128)}, f32[64,512]{1,0:T(8,128)}, f32[1,512]{1,0:T(1,128)}, /*index=5*/f32[80,512]{1,0:T(8,128)}, f32[1,80]{1,0:T(1,128)}) custom-call(f32[8,64]{1,0:T(8,128)} %get-tuple-element.21.refs_0_, f32[64,512]{1,0:T(8,128)} %get-tuple-element.22.refs_1_, ...), custom_call_target="tpu_custom_call" | custom-call | tf_op jit(solution)/shard_map/pallas_call | solution.py:681

commit v6 on v5

--- a/solution.py
+++ b/solution.py
@@ -639,7 +639,7 @@
     return pl.pallas_call(
         functools.partial(score_kernel, members, bands, chunks, part_cols, edge),
         out_shape=tuple(
-            jax.ShapeDtypeStruct(o, single)
+            pltpu.VMEM(o, single)
             for o in (
                 (lat_rows, cols), (rows, hidden), (1, hidden), (rows, hidden), (1, hidden),
                 (channels, hidden), (1, channels),
@@ -666,7 +666,7 @@
             (members * extra, hidden),
         ]]
         + reduce_scratch(members, bands, features, hidden, extra),
-        compiler_params=pltpu.CompilerParams(collective_id=0, has_side_effects=True, vmem_limit_bytes=60 << 20),
+        compiler_params=pltpu.CompilerParams(collective_id=0, has_side_effects=True, vmem_limit_bytes=58 << 20),
     )(latent, *weights, truth, weight)
 
 
@@ -678,6 +678,7 @@
 
 def write_results(values):
     vmem = pl.BlockSpec(memory_space=pltpu.VMEM)
+    values = [pltpu.with_memory_space_constraint(v, pltpu.VMEM) for v in values]
     return pl.pallas_call(
         write_kernel,
         out_shape=tuple(jax.ShapeDtypeStruct(v.shape, v.dtype) for v in values),

time: 98.1 us -> 96.3 us (0.982)
  Pallas kernels: 97.3 us -> 95.5 us
    pallas_call x1, Pallas kernels: 1.81 us -> 0.79 us  [write_results(): pl.pallas_call(write_kernel, out_shape=tuple((jax.ShapeDtypeStruct(v.shap...]
where the time goes in v6:
time: 96.3 us; the launch traced here: 96.1 us
  Pallas kernels  95.5 us (99%)
    pallas_call x1, Pallas kernels, score_and_gradient(): pl.pallas_call(functools.partial(score_kernel, members, bands, chunks, pa...  94.7 us

profile of v6, /device:TPU:0, one launch (start us, length us, event | category | flops | bytes accessed | tf_op | source)
XLA Modules:
  0.0 96.1 jit_solution(17430798111623188406)
XLA Ops:
  0.6 94.7 %shard_map.144 = (f32[8,64]{1,0:T(8,128)S(1)}, f32[64,512]{1,0:T(8,128)S(1)}, f32[1,512]{1,0:T(1,128)S(1)}, f32[64,512]{1,0:T(8,128)S(1)}, f32[1,512]{1,0:T(1,12...) custom-call(bf16[8,512,512]{2,1,0:T(8,128)(2,1)} %bitcast.8, bf16[512,512]{1,0:T(8,128)(2,1)} %first_hbm.1, ...), custom_call_target="tpu_custom_call" | custom-call | tf_op jit(solution)/shard_map/pallas_call | solution.py:639
  95.3 0.8 shard_map.145
